TPU v7x, 512 devices: a whole 4x4x16 slice. The times are simulated.
512 devices in a mesh: guide: 2 (over x_lo), seq: 32 (over x_hi, z), blk: 8 (over y, core).
Axes of the slice: x: 4 (x_hi: 2, x_lo: 2; x = x_hi * 2 + x_lo), y: 4, z: 16, core: 2. Of those that a mesh axis runs over, the one named last changes fastest.
Arguments:
- img_hidden: bfloat16 [2, 2, 2048, 3072], P('guide', None, 'seq', 'blk'), may hold values from -6 to 6
- img_query: bfloat16 [2, 2, 2048, 3072], P('guide', None, 'seq', 'blk')
- img_key: bfloat16 [2, 2, 2048, 3072], P('guide', None, 'seq', 'blk')
- img_value: bfloat16 [2, 2, 2048, 3072], P('guide', None, 'seq', 'blk'), may hold values from -6 to 6
- txt_key: bfloat16 [2, 2, 512, 3072], P('guide', None, 'seq', 'blk'), may hold values from -6 to 6
- txt_value: bfloat16 [2, 2, 512, 3072], P('guide', None, 'seq', 'blk'), may hold values from -6 to 6
- query_gain: float32 [128], replicated
- key_gain: float32 [2, 128], replicated
- gate: float32 [2, 2, 3072], P('guide', None, 'blk'), may hold values from -4 to 4
- proj_weight: bfloat16 [3072, 3072], P('blk'), may hold values from -0.15625 to 0.15625
- proj_bias: float32 [3072], P('blk'), may hold values from -3 to 3
- guidance: float32 [2], replicated, may hold values from 1.5 to 5
- text_len: int32 [2], replicated, may hold values from 1 to 512, as said below
- step_index: int32 [1], replicated, may hold values from 0 to 7
- latent: bfloat16 [2, 2048, 3072], P('guide', 'seq', 'blk'), may hold values from -6 to 6
Outputs:
- guided: bfloat16 [2, 2048, 3072], P('guide', 'seq', 'blk')
- next_state: bfloat16 [2, 2048, 3072], P('guide', 'seq', 'blk')
Inputs may be any that keep to these rules, and one draw needn't show every extreme that they name: `text_len`: some prompt has all 512 text slots live.
All inputs are finite; a program needn't handle non-finite values.
Results may differ from a plain program's by a relative error of at most 0.0095.
Values may be sent and summed in bfloat16 or wider, within the bound.
No kernel may reach another device: no remote copies, remote signals or barrier semaphores. Data moves between devices by JAX's collectives and lax.ppermute only.
A program may use at most 64 MiB of HBM per device.

v0:
```python
import jax
import jax.numpy as jnp
from jax import lax
from jax.sharding import PartitionSpec as P

HD = 128
GRID = 64
STEPS = 8


def rope_angles(positions):
    first = HD // 8
    second = (HD - first) // 2
    freqs = 10000.0 ** (-jnp.arange(0, second, 2).astype(jnp.float32) / second)
    rows = (positions // GRID).astype(jnp.float32)
    cols = (positions % GRID).astype(jnp.float32)
    zeros = jnp.zeros((positions.shape[0], first // 2), jnp.float32)
    return jnp.concatenate([zeros, rows[:, None] * freqs, cols[:, None] * freqs], -1)


def rotate(values, angles):
    pairs = values.reshape(values.shape[:-1] + (HD // 2, 2))
    cosine = jnp.cos(angles)[None, :, None, :]
    sine = jnp.sin(angles)[None, :, None, :]
    first = pairs[..., 0] * cosine - pairs[..., 1] * sine
    second = pairs[..., 0] * sine + pairs[..., 1] * cosine
    return jnp.stack([first, second], -1).reshape(values.shape)


def normed(values, gain_row):
    heads = values.astype(jnp.float32).reshape(
        values.shape[0], values.shape[1], values.shape[2] // HD, HD
    )
    return heads / jnp.sqrt(jnp.mean(heads * heads, -1, keepdims=True) + 1e-06) * gain_row


def shards(
    img_hidden,
    img_query,
    img_key,
    img_value,
    txt_key,
    txt_value,
    query_gain,
    key_gain,
    gate,
    proj_weight,
    proj_bias,
    guidance,
    text_len,
    step_index,
    latent,
):
    prompts = img_query.shape[1]
    img_here = img_query.shape[2]
    txt_here = txt_key.shape[2]
    width_here = img_query.shape[3]
    heads_here = width_here // HD
    slot_here = img_here + txt_here
    positions = lax.axis_index("seq") * img_here + jnp.arange(img_here)
    angles = rope_angles(positions)
    queries = rotate(normed(img_query[0], query_gain), angles).astype(jnp.bfloat16)
    keys_img = rotate(normed(img_key[0], key_gain[0]), angles).astype(jnp.bfloat16)
    keys_txt = normed(txt_key[0], key_gain[1]).astype(jnp.bfloat16)
    keys_local = jnp.concatenate([keys_txt, keys_img], 1).reshape(prompts, slot_here, width_here)
    values_local = jnp.concatenate([txt_value[0], img_value[0]], 1)
    running = jnp.full((prompts, img_here, heads_here), -1e30, jnp.float32)
    key_piece = lax.all_gather(keys_local, "seq", axis=1, tiled=True)
    value_piece = lax.all_gather(values_local, "seq", axis=1, tiled=True)
    count = key_piece.shape[1]
    index = jnp.arange(count)
    device = index // slot_here
    within = index % slot_here
    text_pos = device * txt_here + within
    live = (within >= txt_here)[None, :] | (text_pos[None, :] < text_len[:, None])
    key_heads = key_piece.reshape(prompts, count, heads_here, HD)
    value_heads = value_piece.reshape(prompts, count, heads_here, HD)
    scores = jnp.einsum(
        "pqhd,pkhd->pqhk", queries, key_heads, preferred_element_type=jnp.float32
    ) * HD ** (-0.5)
    mask = live[:, None, None, :]
    scores = jnp.where(mask, scores, -1e30)
    newest = jnp.maximum(running, jnp.max(scores, -1))
    expo = jnp.where(mask, jnp.exp(scores - newest[..., None]), 0.0)
    total = jnp.sum(expo, -1)
    accum = jnp.einsum(
        "pqhk,pkhd->pqhd",
        expo.astype(jnp.bfloat16),
        value_heads,
        preferred_element_type=jnp.float32,
    )
    running, total, accum = (newest, total, accum)
    attn = (accum / total[..., None]).astype(jnp.bfloat16).reshape(prompts * img_here, width_here)
    partial_value = jnp.dot(attn, proj_weight, preferred_element_type=jnp.float32)
    proj = lax.psum_scatter(
        partial_value.astype(jnp.bfloat16), "blk", scatter_dimension=1, tiled=True
    ).astype(jnp.float32)
    proj = (proj + proj_bias).reshape(prompts, img_here, width_here)
    layer_out = (img_hidden[0].astype(jnp.float32) + gate[0][:, None, :] * proj).astype(
        jnp.bfloat16
    )
    both_halves = lax.all_to_all(layer_out[None], "guide", split_axis=1, concat_axis=0, tiled=True)
    cond = both_halves[0].astype(jnp.float32)
    uncond = both_halves[1].astype(jnp.float32)
    own_prompts = cond.shape[0]
    scale_here = lax.dynamic_slice_in_dim(
        guidance, lax.axis_index("guide") * own_prompts, own_prompts, 0
    )
    guided_f = uncond + scale_here[:, None, None] * (cond - uncond)
    index = step_index[0]
    u_now = 1.0 - index.astype(jnp.float32) / STEPS
    u_next = 1.0 - (index + 1).astype(jnp.float32) / STEPS
    step_size = 3.0 * u_next / (1.0 + 2.0 * u_next) - 3.0 * u_now / (1.0 + 2.0 * u_now)
    next_state = (latent.astype(jnp.float32) + step_size * guided_f).astype(jnp.bfloat16)
    return (guided_f.astype(jnp.bfloat16), next_state)


def solution(mesh):
    return jax.shard_map(
        shards,
        mesh=mesh,
        in_specs=(
            P("guide", None, "seq", "blk"),
            P("guide", None, "seq", "blk"),
            P("guide", None, "seq", "blk"),
            P("guide", None, "seq", "blk"),
            P("guide", None, "seq", "blk"),
            P("guide", None, "seq", "blk"),
            P(),
            P(),
            P("guide", None, "blk"),
            P("blk", None),
            P("blk"),
            P(),
            P(),
            P(),
            P("guide", "seq", "blk"),
        ),
        out_specs=(P("guide", "seq", "blk"), P("guide", "seq", "blk")),
        check_vma=False,
    )
```

profile of v0, /device:TPU:4, one launch (start us, length us, event | category | flops | bytes accessed | tf_op | source)
XLA Modules:
  0.0 420.7 jit_solution(10959240967538015908)
XLA Ops:
  7.2 0.6 multiply_power_fusion
  7.8 1.6 convert_multiply_fusion.1
  9.5 1.0 copy.58
  10.5 1.6 convert_multiply_fusion.2
  12.1 1.0 copy.52
  13.1 0.6 fusion.35
  13.7 0.8 slice_bitcast_fusion.2
  14.5 0.1 mul.268
  14.6 1.0 mul.267
  15.6 0.2 reduce_sum.37
  15.9 0.7 copy.54
  16.6 1.0 mul.285
  17.6 0.2 reduce_sum.38
  17.8 0.7 copy.60
  18.5 0.8 mul.286
  19.3 0.7 convert_multiply_fusion
  20.1 0.1 reduce_sum.36
  20.2 0.1 div.91
  20.4 0.2 copy.55
  20.6 0.8 broadcast_multiply_fusion.1
  21.3 0.2 fusion.26
  21.5 1.1 divide_multiply_fusion
  22.7 1.0 subtract_convert_fusion
  23.7 0.5 pad_maximum_fusion
  24.2 0.1 pad_maximum_fusion.1
  24.4 0.8 copy.56
  25.2 0.1 copy.82
  25.4 0.8 copy.83
  26.1 0.8 pad_maximum_fusion.3
  27.0 0.5 pad_maximum_fusion.2
  27.6 0.7 compare_or_fusion
  28.3 161.3 %all-gather.5.cloned.1.call-done = bf16[2,2560,384]{2,0,1:T(2,128)(2,1)} async-done(((bf16[2,80,384]{2,0,1:T(2,128)(2,1)}), bf16[2,2560,384]{2,0,1:T(2,128)(2,1)}) %all-gather.5.cloned.1.call-update) | async-done | bytes 3932176 | tf_op jit(solution)/shard_map/all_gather | solution.py:68
  189.6 10.5 %copy.57 = bf16[2,2560,384]{1,2,0:T(8,128)(2,1)} copy(bf16[2,2560,384]{2,0,1:T(2,128)(2,1)} %all-gather.5.cloned.1.call-done) | data formatting | bytes 7864320 | tf_op jit(solution)/shard_map/all_gather | solution.py:68
  200.1 3.2 fusion.38
  203.4 1.9 copy-done.1
  205.2 0.9 fusion.2
  206.1 143.7 %all-gather.3.cloned.1.call-done = bf16[2,2560,384]{2,0,1:T(2,128)(2,1)} async-done(((bf16[2,80,384]{2,0,1:T(2,128)(2,1)}), bf16[2,2560,384]{2,0,1:T(2,128)(2,1)}) %all-gather.3.cloned.1.call-update) | async-done | bytes 3932176 | tf_op jit(solution)/shard_map/all_gather | solution.py:69
  349.8 10.5 %copy.51 = bf16[2,2560,384]{1,2,0:T(8,128)(2,1)} copy(bf16[2,2560,384]{2,0,1:T(2,128)(2,1)} %all-gather.3.cloned.1.call-done) | data formatting | bytes 7864320 | tf_op jit(solution)/shard_map/all_gather | solution.py:69
  360.3 4.8 %fusion.15 = bf16[2,64,3,128]{3,1,2,0:T(8,128)(2,1)S(1)} fusion(bf16[2,2560,3,128]{1,3,2,0:T(8,128)(2,1)} %bitcast.73, f32[2,64,3,2560]{3,1,2,0:T(8,128)} %copy-done.1, f32[2,64,3]{1,2,0:T(4,128)S(1)} %broadcast_maximum_fusion, pred[2,2560]{1,0:T(4,128)(4,1)S(1)} %compare_or_fusion, f32[2,64,3]{1,2,0:T(4,128)S(1)} %fusion.2), kind=kOutput, calls=%fused_computation.13 | convolution fusion | flops 254705664 | bytes 7970816 | tf_op jit(solution)/shard_map/pqhk,pkhd->pqhd/dot_general | solution.py:86
  365.3 0.6 convolution_convert_fusion
  365.9 1.2 copy.69
  367.1 36.4 %reduce-scatter.4.cloned.1.call-done = bf16[384,128]{1,0:T(8,128)(2,1)} async-done(((bf16[3072,128]{1,0:T(8,128)(2,1)}), bf16[384,128]{1,0:T(8,128)(2,1)}) %reduce-scatter.4.cloned.1.call-update) | async-done | bytes 98320
  403.5 1.0 copy.70
  404.5 0.7 add_convert_fusion
  405.2 3.3 all-to-all-start
  409.2 0.6 dynamic_slice.3
  409.9 2.9 all-to-all-done
  412.8 1.3 add_convert_fusion.3
  (37 shorter events, 0.5 us)
Async XLA Ops:
  7.2 358.1 %copy-start = (bf16[384,3072]{1,0:T(8,128)(2,1)S(1)}, bf16[384,3072]{1,0:T(8,128)(2,1)}, u32[]{:S(2)}) copy-start(bf16[384,3072]{1,0:T(8,128)(2,1)} %param.24) | copy-start | bytes 7077892
  7.2 13.2 %copy-start.4 = (bf16[1,2,16,384]{3,2,1,0:T(8,128)(2,1)S(1)}, bf16[1,2,16,384]{3,2,1,0:T(8,128)(2,1)}, u32[]{:S(2)}) copy-start(bf16[1,2,16,384]{3,2,1,0:T(8,128)(2,1)} %param.19) | copy-start | bytes 73732
  7.2 182.4 %all-gather.5.cloned.1.call-start = ((), (), s32[]{:S(2)}) async-start(), calls=%async_computation.3 | async-start | bytes 4055040 | tf_op jit(solution)/shard_map/all_gather | solution.py:68
  17.8 7.4 %copy-start.2 = (bf16[1,2,64,384]{3,2,1,0:T(8,128)(2,1)S(1)}, bf16[1,2,64,384]{3,2,1,0:T(8,128)(2,1)}, u32[]{:S(2)}) copy-start(bf16[1,2,64,384]{3,2,1,0:T(8,128)(2,1)} %param.18) | copy-start | bytes 294916
  25.2 324.6 %all-gather.3.cloned.1.call-start = ((), (), s32[]{:S(2)}) async-start(), calls=%async_computation.2 | async-start | bytes 4055040 | tf_op jit(solution)/shard_map/all_gather | solution.py:69
  27.0 376.5 %reduce-scatter.4.cloned.1.call-start = ((), (), s32[]{:S(2)}) async-start(), calls=%async_computation.4 | async-start | bytes 884736
  203.3 1.9 copy-start.1
  365.1 39.4 %copy-start.7 = (f32[384]{0:T(512)S(1)}, f32[384]{0:T(512)}, u32[]{:S(2)}) copy-start(f32[384]{0:T(512)} %param.25) | copy-start | bytes 4612
  365.1 39.4 %copy-start.3 = (bf16[1,2,64,384]{3,2,1,0:T(8,128)(2,1)S(1)}, bf16[1,2,64,384]{3,2,1,0:T(8,128)(2,1)}, u32[]{:S(2)}) copy-start(bf16[1,2,64,384]{3,2,1,0:T(8,128)(2,1)} %param.15) | copy-start | bytes 294916
  365.2 39.4 %copy-start.6 = (f32[1,2,384]{2,1,0:T(2,128)S(1)}, f32[1,2,384]{2,1,0:T(2,128)}, u32[]{:S(2)}) copy-start(f32[1,2,384]{2,1,0:T(2,128)} %param.23) | copy-start | bytes 9220
  365.2 44.1 %copy-start.8 = (f32[2]{0:T(128)S(1)}, f32[2]{0:T(128)}, u32[]{:S(2)}) copy-start(f32[2]{0:T(128)} %param.26) | copy-start | bytes 28
  365.2 47.7 %copy-start.5 = (bf16[1,64,384]{2,1,0:T(8,128)(2,1)S(1)}, bf16[1,64,384]{2,1,0:T(8,128)(2,1)}, u32[]{:S(2)}) copy-start(bf16[1,64,384]{2,1,0:T(8,128)(2,1)} %param.29) | copy-start | bytes 147460
  405.2 7.6 %all-to-all-start = ((bf16[1,2,64,384]{3,2,0,1:T(8,128)(2,1)}), bf16[1,2,64,384]{3,2,0,1:T(8,128)(2,1)S(1)}, u32[]{:S(2)}, u32[]{:S(2)}) async-start(bf16[1,2,64,384]{3,2,0,1:T(8,128)(2,1)} %add_convert_fusion), calls=%async_computation | async-start | bytes 196608 | tf_op jit(solution)/shard_map/all_to_all | solution.py:102
Sparse Core Ops, SparseCore 0:
  25.3 164.2 all-gather.4
  192.7 157.0 all-gather.2
  367.2 36.2 reduce-scatter.3
where the time goes:
time: 422 us; the launch traced here: 421 us
  waiting for transfers between devices  344 us (82%)
  local copies, waits for them, and re-layouts  35 us (8%)
  between operations  14.9 us (4%)
  other arithmetic  14.5 us (3%)
  matrix products  8.61 us (2%)
    all_gather x1, waiting for transfers between devices, shards(): key_piece = lax.all_gather(keys_local, 'seq', axis=1, tiled=True)  161 us
    all_gather x1, waiting for transfers between devices, shards(): value_piece = lax.all_gather(values_local, 'seq', axis=1, tiled=True)  144 us
    unnamed x4, waiting for transfers between devices  36.5 us
    all_gather x1, local copies, waits for them, and re-layouts, shards(): value_piece = lax.all_gather(values_local, 'seq', axis=1, tiled=True)  10.5 us
    all_gather x1, local copies, waits for them, and re-layouts, shards(): key_piece = lax.all_gather(keys_local, 'seq', axis=1, tiled=True)  10.5 us
  transfers between devices with their start and end apart: 4, of which 4 were waited for; matrix products, arithmetic and copies ran while one was open for 4% of the time, Pallas kernels for 0%

commit v1 on v0

--- a/solution.py
+++ b/solution.py
@@ -66,7 +66,9 @@
     values_local = jnp.concatenate([txt_value[0], img_value[0]], 1)
     running = jnp.full((prompts, img_here, heads_here), -1e30, jnp.float32)
     key_piece = lax.all_gather(keys_local, "seq", axis=1, tiled=True)
-    value_piece = lax.all_gather(values_local, "seq", axis=1, tiled=True)
+    value_piece = jnp.concatenate(
+        lax.all_to_all(jnp.stack([values_local] * lax.axis_size("seq")), "seq", 0, 0), axis=1
+    )
     count = key_piece.shape[1]
     index = jnp.arange(count)
     device = index // slot_here

time: 422 us -> 347 us (0.82)
  waiting for transfers between devices: 344 us -> 257 us
  starting transfers between devices: 3.46 us -> 21.8 us
  other arithmetic: 14.5 us -> 8.19 us
    all_gather x1 -> x0, waiting for transfers between devices: 144 us -> none  [shards(): value_piece = lax.all_gather(values_local, 'seq', axis=1, tiled=True)]
    all_gather x1, waiting for transfers between devices: 161 us -> 218 us  [shards(): key_piece = lax.all_gather(keys_local, 'seq', axis=1, tiled=True)]
    all_to_all x0 -> x1, starting transfers between devices: none -> 18.4 us  [shards(): lax.all_to_all(jnp.stack([values_local] * lax.axis_size('seq')), 'seq', 0...]
    another operation x0 -> x2, local copies, waits for them, and re-layouts: none -> 13.1 us  [the longest x1 10.9 us: shards(): value_heads = value_piece.reshape(prompts, count, heads_here, HD)]
    all_gather x1 -> x0, local copies, waits for them, and re-layouts: 10.5 us -> none  [shards(): value_piece = lax.all_gather(values_local, 'seq', axis=1, tiled=True)]
    reshape x0 -> x1, local copies, waits for them, and re-layouts: none -> 4.45 us  [shards(): jnp.concatenate(lax.all_to_all(jnp.stack([values_local] * lax.axis_size('...]
    unnamed x4 -> x3, waiting for transfers between devices: 36.5 us -> 36.2 us
  transfers between devices with their start and end apart: 4 -> 4, of which waited for: 4 -> 3; matrix products, arithmetic and copies ran while one was open for 4% -> 6% of each run, Pallas kernels for 0% -> 0%
where the time goes in v1:
time: 347 us; the launch traced here: 346 us
  waiting for transfers between devices  257 us (74%)
  local copies, waits for them, and re-layouts  35.9 us (10%)
  starting transfers between devices  21.8 us (6%)
  between operations  15.2 us (4%)
  matrix products  8.61 us (2%)
  other arithmetic  8.19 us (2%)
    all_gather x1, waiting for transfers between devices, shards(): key_piece = lax.all_gather(keys_local, 'seq', axis=1, tiled=True)  218 us
    unnamed x3, waiting for transfers between devices  36.2 us
    all_to_all x1, starting transfers between devices, shards(): lax.all_to_all(jnp.stack([values_local] * lax.axis_size('seq')), 'seq', 0...  18.4 us
    another operation x1, local copies, waits for them, and re-layouts, shards(): value_heads = value_piece.reshape(prompts, count, heads_here, HD)  10.9 us
    all_gather x1, local copies, waits for them, and re-layouts, shards(): key_piece = lax.all_gather(keys_local, 'seq', axis=1, tiled=True)  10.6 us
  transfers between devices with their start and end apart: 4, of which 3 were waited for; matrix products, arithmetic and copies ran while one was open for 6% of the time, Pallas kernels for 0%

profile of v1, /device:TPU:4, one launch (start us, length us, event | category | flops | bytes accessed | tf_op | source)
XLA Modules:
  0.0 346.4 jit_solution(17675082361574705458)
XLA Ops:
  7.2 1.1 pad_maximum_fusion.3
  8.2 2.2 stack.8
  10.5 18.4 %all-to-all-start = ((bf16[32,2,80,384]{3,2,1,0:T(8,128)(2,1)}), bf16[32,2,80,384]{3,2,1,0:T(8,128)(2,1)}, u32[]{:S(2)}, u32[]{:S(2)}) async-start(bf16[32,2,80,384]{3,2,1,0:T(8,128)(2,1)} %stack.8), calls=%async_computation | async-start | bytes 7864320 | tf_op jit(solution)/shard_map/all_to_all | solution.py:70
  28.9 0.0 all-gather.2.cloned.1.call-start
  29.0 0.1 mul.268
  29.1 0.1 copy.46
  29.3 0.1 mul.267
  29.4 0.2 reduce_sum.37
  29.7 0.1 copy.48
  29.7 0.1 copy.52
  29.9 0.7 convert_multiply_fusion.1
  30.6 1.0 mul.285
  31.6 0.2 reduce_sum.38
  31.9 0.1 copy.54
  31.9 0.1 mul.286
  32.1 0.1 reduce_sum.36
  32.3 0.1 div.91
  32.4 0.2 copy.49
  32.7 0.1 broadcast_multiply_fusion.1
  32.7 0.2 fusion.33
  32.9 0.4 divide_multiply_fusion
  33.4 1.0 subtract_convert_fusion
  34.4 0.5 pad_maximum_fusion
  34.9 0.1 pad_maximum_fusion.1
  35.1 0.8 copy.50
  35.9 0.0 all-gather.2.cloned.1.call-update
  35.9 0.0 reduce-scatter.4.cloned.1.call-start
  36.0 0.5 pad_maximum_fusion.2
  36.5 0.1 compare_or_fusion
  36.6 217.5 %all-gather.2.cloned.1.call-done = bf16[2,2560,384]{2,0,1:T(2,128)(2,1)} async-done(((bf16[2,80,384]{2,0,1:T(2,128)(2,1)}), bf16[2,2560,384]{2,0,1:T(2,128)(2,1)}) %all-gather.2.cloned.1.call-update) | async-done | bytes 3932176 | tf_op jit(solution)/shard_map/all_gather | solution.py:68
  254.2 10.6 %copy.51 = bf16[2,2560,384]{1,2,0:T(8,128)(2,1)} copy(bf16[2,2560,384]{2,0,1:T(2,128)(2,1)} %all-gather.2.cloned.1.call-done) | data formatting | bytes 7864320 | tf_op jit(solution)/shard_map/all_gather | solution.py:68
  264.7 3.2 fusion.45
  268.0 2.0 copy-done.1
  269.9 0.9 fusion.4
  270.8 4.5 %copy.45 = bf16[2,32,80,384]{3,2,1,0:T(8,128)(2,1)} copy(bf16[2,32,80,384]{3,2,0,1:T(8,128)(2,1)} %bitcast.4) | data formatting | bytes 7864320 | tf_op jit(solution)/shard_map/reshape | solution.py:69
  275.2 10.9 %reshape_reshape.3 = bf16[2,2560,3,128]{3,2,1,0:T(4,128)(2,1)} reshape(bf16[2,32,80,384]{3,2,1,0:T(8,128)(2,1)} %copy.45) | data formatting | bytes 7864320 | tf_op jit(solution)/shard_map/reshape;reshape | solution.py:79
  286.1 4.8 %fusion.20 = bf16[2,64,3,128]{3,1,2,0:T(8,128)(2,1)S(1)} fusion(bf16[2,2560,3,128]{3,2,1,0:T(4,128)(2,1)} %reshape_reshape.3, f32[2,64,3,2560]{3,1,2,0:T(8,128)} %copy-done.1, f32[2,64,3]{1,2,0:T(4,128)S(1)} %broadcast_maximum_fusion, pred[2,2560]{1,0:T(4,128)(4,1)S(1)} %compare_or_fusion, f32[2,64,3]{1,2,0:T(4,128)S(1)} %fusion.4), kind=kOutput, calls=%fused_computation.14 | convolution fusion | flops 254705664 | bytes 7970816 | tf_op jit(solution)/shard_map/pqhk,pkhd->pqhd/dot_general | solution.py:88
  291.0 0.1 copy.58
  291.1 0.6 convolution_convert_fusion
  291.7 1.2 copy.62
  292.8 0.0 reduce-scatter.4.cloned.1.call-update
  292.8 36.2 %reduce-scatter.4.cloned.1.call-done = bf16[384,128]{1,0:T(8,128)(2,1)} async-done(((bf16[3072,128]{1,0:T(8,128)(2,1)}), bf16[384,128]{1,0:T(8,128)(2,1)}) %reduce-scatter.4.cloned.1.call-update) | async-done | bytes 98320
  329.0 1.0 copy.63
  330.1 0.7 add_convert_fusion
  330.7 3.3 all-to-all-start.1
  334.8 0.6 dynamic_slice.3
  335.4 3.0 all-to-all-done.1
  338.4 1.2 add_convert_fusion.3
  (44 shorter events, 0.3 us)
Async XLA Ops:
  7.2 283.9 %copy-start = (bf16[384,3072]{1,0:T(8,128)(2,1)S(1)}, bf16[384,3072]{1,0:T(8,128)(2,1)}, u32[]{:S(2)}) copy-start(bf16[384,3072]{1,0:T(8,128)(2,1)} %param.24) | copy-start | bytes 7077892
  10.5 18.5 %copy-start.9 = (f32[2,128]{1,0:T(2,128)S(1)}, f32[2,128]{1,0:T(2,128)}, u32[]{:S(2)}) copy-start(f32[2,128]{1,0:T(2,128)} %param.22) | copy-start | bytes 3076
  10.5 18.7 %copy-start.2 = (bf16[1,2,64,384]{3,2,1,0:T(8,128)(2,1)S(1)}, bf16[1,2,64,384]{3,2,1,0:T(8,128)(2,1)}, u32[]{:S(2)}) copy-start(bf16[1,2,64,384]{3,2,1,0:T(8,128)(2,1)} %param.17) | copy-start | bytes 294916
  10.5 19.3 %copy-start.3 = (bf16[1,2,64,384]{3,2,1,0:T(8,128)(2,1)S(1)}, bf16[1,2,64,384]{3,2,1,0:T(8,128)(2,1)}, u32[]{:S(2)}) copy-start(bf16[1,2,64,384]{3,2,1,0:T(8,128)(2,1)} %param.16) | copy-start | bytes 294916
  10.5 21.5 %copy-start.10 = (f32[128]{0:T(128)S(1)}, f32[128]{0:T(128)}, u32[]{:S(2)}) copy-start(f32[128]{0:T(128)} %param.21) | copy-start | bytes 1540
  10.5 21.6 %copy-start.5 = (bf16[1,2,16,384]{3,2,1,0:T(8,128)(2,1)S(1)}, bf16[1,2,16,384]{3,2,1,0:T(8,128)(2,1)}, u32[]{:S(2)}) copy-start(bf16[1,2,16,384]{3,2,1,0:T(8,128)(2,1)} %param.19) | copy-start | bytes 73732
  10.5 260.3 %all-to-all-start = ((bf16[32,2,80,384]{3,2,1,0:T(8,128)(2,1)}), bf16[32,2,80,384]{3,2,1,0:T(8,128)(2,1)}, u32[]{:S(2)}, u32[]{:S(2)}) async-start(bf16[32,2,80,384]{3,2,1,0:T(8,128)(2,1)} %stack.8), calls=%async_computation | async-start | bytes 7864320 | tf_op jit(solution)/shard_map/all_to_all | solution.py:70
  28.9 225.3 %all-gather.2.cloned.1.call-start = ((), (), s32[]{:S(2)}) async-start(), calls=%async_computation.3 | async-start | bytes 4055040 | tf_op jit(solution)/shard_map/all_gather | solution.py:68
  29.9 6.6 %copy-start.11 = (s32[2]{0:T(128)S(1)}, s32[2]{0:T(128)}, u32[]{:S(2)}) copy-start(s32[2]{0:T(128)} %param.27) | copy-start | bytes 28
  35.9 293.1 %reduce-scatter.4.cloned.1.call-start = ((), (), s32[]{:S(2)}) async-start(), calls=%async_computation.4 | async-start | bytes 884736
  267.9 2.0 copy-start.1
  290.9 39.1 %copy-start.8 = (f32[384]{0:T(512)S(1)}, f32[384]{0:T(512)}, u32[]{:S(2)}) copy-start(f32[384]{0:T(512)} %param.25) | copy-start | bytes 4612
  290.9 39.1 %copy-start.4 = (bf16[1,2,64,384]{3,2,1,0:T(8,128)(2,1)S(1)}, bf16[1,2,64,384]{3,2,1,0:T(8,128)(2,1)}, u32[]{:S(2)}) copy-start(bf16[1,2,64,384]{3,2,1,0:T(8,128)(2,1)} %param.15) | copy-start | bytes 294916
  290.9 39.1 %copy-start.7 = (f32[1,2,384]{2,1,0:T(2,128)S(1)}, f32[1,2,384]{2,1,0:T(2,128)}, u32[]{:S(2)}) copy-start(f32[1,2,384]{2,1,0:T(2,128)} %param.23) | copy-start | bytes 9220
  291.0 43.8 %copy-start.12 = (f32[2]{0:T(128)S(1)}, f32[2]{0:T(128)}, u32[]{:S(2)}) copy-start(f32[2]{0:T(128)} %param.26) | copy-start | bytes 28
  291.0 47.4 %copy-start.6 = (bf16[1,64,384]{2,1,0:T(8,128)(2,1)S(1)}, bf16[1,64,384]{2,1,0:T(8,128)(2,1)}, u32[]{:S(2)}) copy-start(bf16[1,64,384]{2,1,0:T(8,128)(2,1)} %param.29) | copy-start | bytes 147460
  330.7 7.6 %all-to-all-start.1 = ((bf16[1,2,64,384]{3,2,0,1:T(8,128)(2,1)}), bf16[1,2,64,384]{3,2,0,1:T(8,128)(2,1)S(1)}, u32[]{:S(2)}, u32[]{:S(2)}) async-start(bf16[1,2,64,384]{3,2,0,1:T(8,128)(2,1)} %add_convert_fusion), calls=%async_computation.1 | async-start | bytes 196608 | tf_op jit(solution)/shard_map/all_to_all | solution.py:104
Sparse Core Ops, SparseCore 0:
  36.0 218.0 all-gather.1
  293.0 35.9 reduce-scatter.3
